TPU v7x, 32 devices: a whole 2x2x4 slice. The times are simulated.
32 devices in a mesh: section: 4 (over y, core), expert: 8 (over z, x).
Axes of the slice: x: 2, y: 2, z: 4, core: 2. Of those that a mesh axis runs over, the one named last changes fastest.
Arguments:
- token_ids: int32 [4, 128], replicated, may hold values from 0 to 75967
- embed_table: bfloat16 [75968, 2048], P('section', 'expert'), may hold values from -6 to 6
- attn_gain: float32 [4, 2048], P('section'), may hold values from 0.5 to 1.5
- moe_gain: float32 [4, 2048], P('section'), may hold values from 0.5 to 1.5
- query_gain: float32 [4, 32, 128], P('section'), may hold values from 0.1 to 1.9
- key_gain: float32 [4, 2, 128], P('section'), may hold values from 0.1 to 1.9
- key_cache: bfloat16 [4, 128, 128, 256], P('section', 'expert'), may hold values from -210 to 210
- value_cache: bfloat16 [4, 128, 128, 256], P('section', 'expert'), may hold values from -3 to 3
- cache_len: int32 [128], P('expert'), may hold values from 1 to 128, 8192 in all
- expert_ids: int32 [4, 4, 128, 4], P('section'), may hold values from 0 to 7, all different within a row; in each aligned block of 4 rows (0 to 3, 4 to 7, ..., all dimensions but the last counted through in order) at most 4 rows name the same one
- route_raw: float32 [4, 4, 128, 4], P('section'), may hold values from 0.1 to 1
- gate_weights: bfloat16 [4, 8, 2048, 768], P('section', 'expert'), may hold values from -0.125 to 0.125
- up_weights: bfloat16 [4, 8, 2048, 768], P('section', 'expert'), may hold values from -0.125 to 0.125
- down_weights: bfloat16 [4, 8, 768, 2048], P('section', 'expert'), may hold values from -0.21875 to 0.21875
Outputs:
- hidden: bfloat16 [4, 4, 128, 2048], P('section', None, 'expert')
Inputs may be any that keep to these rules, and one draw needn't show every extreme that they name: `expert_ids`: in each layer and step, at most 4 of the rows of one aligned block of 4 rows name one expert, a bound that some block reaches of them. `cache_len`: some row holds 128 entries.
All inputs are finite; a program needn't handle non-finite values. No bound on the sum of `cache_len` on one device may be relied on, other than what follows from the above.
Results may differ from a plain program's by a relative error of at most 0.02.
Values may be sent and summed in bfloat16 or wider, within the bound.
A program may use at most 64 MiB of HBM per device.

v0:
```python
import math

import jax
import jax.numpy as jnp
from jax import lax
from jax.sharding import PartitionSpec as P

BLOCK = 4


eps = 1e-06


def passed_along(x, axis, by):
    devices = lax.axis_size(axis)
    pairs = [(i, i + by) for i in range(devices) if 0 <= i + by < devices]
    return lax.ppermute(x, axis, pairs)


def rms_scale(values):
    return lax.rsqrt(jnp.mean(values * values, axis=-1, keepdims=True) + eps)


def expert_block(rows_in, gate_matrix, up_matrix, down_matrix):
    gate_part = jnp.dot(rows_in, gate_matrix, preferred_element_type=jnp.float32)
    lifted = jnp.dot(rows_in, up_matrix, preferred_element_type=jnp.float32)
    activated = (jax.nn.silu(gate_part) * lifted).astype(jnp.bfloat16)
    return jnp.dot(activated, down_matrix, preferred_element_type=jnp.float32).astype(jnp.bfloat16)


def attend(queries, key_rows, value_rows, near_keys, near_values, lengths, step_at):
    row_count, kv_heads, blocks, head_size = queries.shape
    cache_size = key_rows.shape[1]
    step_total = near_keys.shape[0]
    score_scale = 1.0 / math.sqrt(head_size)
    key_grid = key_rows.reshape(row_count, cache_size, kv_heads, head_size)
    value_grid = value_rows.reshape(row_count, cache_size, kv_heads, head_size)
    near_key_grid = near_keys.reshape(step_total, row_count, kv_heads, head_size)
    near_value_grid = near_values.reshape(step_total, row_count, kv_heads, head_size)
    far_scores = (
        jnp.einsum("rgjd,rcgd->rgjc", queries, key_grid, preferred_element_type=jnp.float32)
        * score_scale
    )
    near_scores = (
        jnp.einsum("rgjd,srgd->rgjs", queries, near_key_grid, preferred_element_type=jnp.float32)
        * score_scale
    )
    far_allowed = (jnp.arange(cache_size)[None, :] < lengths[:, None])[:, None, None, :]
    near_allowed = (jnp.arange(step_total) <= step_at)[None, None, None, :]
    far_scores = jnp.where(far_allowed, far_scores, -1e30)
    near_scores = jnp.where(near_allowed, near_scores, -1e30)
    row_top = jnp.maximum(
        jnp.max(far_scores, axis=-1, keepdims=True), jnp.max(near_scores, axis=-1, keepdims=True)
    )
    far_exp = jnp.where(far_allowed, jnp.exp(far_scores - row_top), 0.0)
    near_exp = jnp.where(near_allowed, jnp.exp(near_scores - row_top), 0.0)
    denominator = jnp.sum(far_exp, axis=-1, keepdims=True) + jnp.sum(
        near_exp, axis=-1, keepdims=True
    )
    far_probs = (far_exp / denominator).astype(jnp.bfloat16)
    near_probs = (near_exp / denominator).astype(jnp.bfloat16)
    far_part = jnp.einsum(
        "rgjc,rcgd->rgjd", far_probs, value_grid, preferred_element_type=jnp.float32
    )
    near_part = jnp.einsum(
        "rgjs,srgd->rgjd", near_probs, near_value_grid, preferred_element_type=jnp.float32
    )
    return far_part + near_part


def on_device(
    token_ids,
    embed_table,
    attn_gain,
    moe_gain,
    query_gain,
    key_gain,
    key_cache,
    value_cache,
    cache_len,
    expert_ids,
    route_raw,
    gate_weights,
    up_weights,
    down_weights,
):
    section_count = lax.axis_size("section")
    expert_count = lax.axis_size("expert")
    section_at = lax.axis_index("section")
    owner_at = lax.axis_index("expert")
    step_total, all_rows = token_ids.shape
    vocab_part = embed_table.shape[0]
    row_count = all_rows // expert_count
    model_width = attn_gain.shape[1]
    local_layers = gate_weights.shape[0]
    head_size = query_gain.shape[2]
    kv_heads = key_gain.shape[1]
    blocks = model_width // head_size
    top_count = expert_ids.shape[3]
    bucket_cap = 2 * BLOCK * top_count // expert_count
    kv_width = kv_heads * head_size
    shifted = token_ids - section_at * vocab_part
    inside = (shifted >= 0) & (shifted < vocab_part)
    looked = jnp.take(embed_table, jnp.clip(shifted, 0, vocab_part - 1), axis=0)
    looked = jnp.where(inside[:, :, None], looked, jnp.zeros_like(looked))
    owned_rows = lax.all_to_all(looked, "expert", split_axis=1, concat_axis=2, tiled=True)
    embedded = lax.psum(owned_rows.astype(jnp.float32).astype(jnp.bfloat16), "section")
    groups = 1
    group_rows = row_count // groups
    item_count = step_total * groups
    slot_count = min(group_rows // BLOCK * bucket_cap, group_rows)
    total_slots = item_count + section_count - 1

    def expert_mix(layer_at, routed, step_at, first_row):
        base_row = owner_at * row_count + first_row
        chosen_ids = lax.dynamic_slice(
            expert_ids, (layer_at, step_at, base_row, 0), (1, 1, group_rows, top_count)
        )[0, 0]
        raw_weights = lax.dynamic_slice(
            route_raw, (layer_at, step_at, base_row, 0), (1, 1, group_rows, top_count)
        )[0, 0]
        weights = raw_weights / jnp.sum(raw_weights, axis=-1, keepdims=True)
        expert_iota = jnp.arange(expert_count, dtype=jnp.int32)
        matches = chosen_ids[:, :, None] == expert_iota[None, None, :]
        member = jnp.any(matches, axis=1)
        shares = jnp.sum(jnp.where(matches, weights[:, :, None], 0.0), axis=1)
        places = jnp.cumsum(member.astype(jnp.int32), axis=0) - 1
        slot_iota = jnp.arange(slot_count, dtype=jnp.int32)
        packing = (member[None, :, :] & (places[None, :, :] == slot_iota[:, None, None])).astype(
            jnp.bfloat16
        )
        outgoing = jnp.einsum(
            "sre,rd->esd", packing, routed, preferred_element_type=jnp.float32
        ).astype(jnp.bfloat16)
        arrived = lax.all_to_all(outgoing, "expert", split_axis=0, concat_axis=0, tiled=True)
        source_count, item_total, feature_count = arrived.shape
        flattened = arrived.reshape(source_count * item_total, feature_count)
        served_flat = expert_block(
            flattened, gate_weights[layer_at, 0], up_weights[layer_at, 0], down_weights[layer_at, 0]
        )
        served = served_flat.reshape(source_count, item_total, feature_count)
        returned = lax.all_to_all(served, "expert", split_axis=0, concat_axis=0, tiled=True)
        unpacked = jnp.einsum("sre,esd->red", packing, returned, preferred_element_type=jnp.float32)
        return jnp.einsum("re,red->rd", shares, unpacked)

    def one_layer(layer_at, hidden_now, fresh_keys, fresh_values, step_at, first_row, active):
        hidden_wide = hidden_now.astype(jnp.float32)
        scaled = hidden_wide * rms_scale(hidden_wide) * attn_gain[layer_at]
        pieces = scaled.reshape(group_rows, blocks, head_size)
        normed = pieces * rms_scale(pieces)
        queries = (
            normed[:, None] * query_gain[layer_at].reshape(kv_heads, blocks, head_size)
        ).astype(jnp.bfloat16)
        key_new = (
            (normed[:, :kv_heads] * key_gain[layer_at])
            .astype(jnp.bfloat16)
            .reshape(group_rows, kv_width)
        )
        value_new = (
            pieces[:, kv_heads : 2 * kv_heads].astype(jnp.bfloat16).reshape(group_rows, kv_width)
        )
        corner = (layer_at, step_at, first_row, 0)
        old_keys = lax.dynamic_slice(fresh_keys, corner, (1, 1, group_rows, kv_width))
        old_values = lax.dynamic_slice(fresh_values, corner, (1, 1, group_rows, kv_width))
        fresh_keys = lax.dynamic_update_slice(
            fresh_keys, jnp.where(active, key_new[None, None], old_keys), corner
        )
        fresh_values = lax.dynamic_update_slice(
            fresh_values, jnp.where(active, value_new[None, None], old_values), corner
        )
        key_rows = key_cache[0]
        value_rows = value_cache[0]
        near_keys = fresh_keys[0]
        near_values = fresh_values[0]
        head_out = attend(queries, key_rows, value_rows, near_keys, near_values, cache_len, step_at)
        mid = hidden_wide + jnp.sum(head_out, axis=1).reshape(group_rows, model_width)
        routed = (mid * rms_scale(mid) * moe_gain[layer_at]).astype(jnp.bfloat16)
        mixture = expert_mix(layer_at, routed, step_at, first_row)
        return ((mid + mixture).astype(jnp.bfloat16), fresh_keys, fresh_values)

    def run_slot(slot_at, state):
        inflow, fresh_keys, fresh_values, outputs = state
        item_at = slot_at - section_at
        active = (item_at >= 0) & (item_at < item_count)
        item_at = jnp.clip(item_at, 0, item_count - 1)
        step_at = item_at // groups
        first_row = item_at % groups * group_rows
        start_rows = lax.dynamic_slice(
            embedded, (step_at, first_row, 0), (1, group_rows, model_width)
        )[0]
        hidden_now = jnp.where(section_at == 0, start_rows, inflow)
        hidden_now, fresh_keys, fresh_values = one_layer(
            0, hidden_now, fresh_keys, fresh_values, step_at, first_row, active
        )
        corner = (0, step_at, first_row, 0)
        current = lax.dynamic_slice(outputs, corner, (1, 1, group_rows, model_width))
        outputs = lax.dynamic_update_slice(
            outputs, jnp.where(active, hidden_now[None, None], current), corner
        )
        inflow = passed_along(hidden_now, "section", 1)
        return (inflow, fresh_keys, fresh_values, outputs)

    start_state = (
        jnp.zeros((group_rows, model_width), jnp.bfloat16),
        jnp.zeros((local_layers, step_total, row_count, kv_width), jnp.bfloat16),
        jnp.zeros((local_layers, step_total, row_count, kv_width), jnp.bfloat16),
        jnp.zeros((local_layers, step_total, row_count, model_width), jnp.bfloat16),
    )
    final_state = lax.fori_loop(0, total_slots, run_slot, start_state)
    return final_state[3]


def solution(mesh):
    in_specs = (
        P(),
        P("section", "expert"),
        P("section", None),
        P("section", None),
        P("section", None, None),
        P("section", None, None),
        P("section", "expert", None, None),
        P("section", "expert", None, None),
        P("expert"),
        P("section", None, None, None),
        P("section", None, None, None),
        P("section", "expert", None, None),
        P("section", "expert", None, None),
        P("section", "expert", None, None),
    )
    out_specs = P("section", None, "expert", None)
    return jax.shard_map(
        on_device, mesh=mesh, in_specs=in_specs, out_specs=out_specs, check_vma=False
    )
```

profile of v0, /device:TPU:0, one launch (start us, length us, event | category | flops | bytes accessed | tf_op | source)
XLA Modules:
  0.0 517.2 jit_solution(6446920938057071880)
XLA Ops:
  8.2 6.6 %gather_fusion = bf16[512,256]{1,0:T(8,128)(2,1)S(1)} fusion(bf16[18992,256]{1,0:T(8,128)(2,1)} %param.17, s32[1024]{0:T(1024)S(1)} %pad_clamp_fusion), kind=kCustom, calls=%fused_computation | custom fusion | bytes 526336 | tf_op jit(solution)/shard_map/jit(_take)/gather | solution.py:104
  15.3 16.2 %all_to_all.48 = bf16[4,128,256]{2,0,1:T(4,128)(2,1)S(1)} all-to-all(bf16[4,128,256]{2,0,1:T(4,128)(2,1)S(1)} %fusion.71), channel_id=1, replica_groups=mesh['section'=4,'expert'=8] {'expert'}, dimensions={1} | all-to-all | bytes 524288 | tf_op jit(solution)/shard_map/all_to_all | solution.py:106
  32.5 2.2 squeeze.100
  34.7 2.2 squeeze.99
  36.9 26.8 %all-reduce.2.cloned.1.call-done = bf16[4,16,2048]{2,1,0:T(8,128)(2,1)} async-done(((bf16[4,16,2048]{2,1,0:T(8,128)(2,1)}), bf16[4,16,2048]{2,1,0:T(8,128)(2,1)}) %all-reduce.2.cloned.1.call-update) | async-done | bytes 262160 | tf_op jit(solution)/shard_map/psum | solution.py:107
  65.6 444.7 %while.23 = (s32[]{:T(128)}, bf16[16,2048]{1,0:T(8,128)(2,1)S(1)}, bf16[1,4,16,256]{3,2,1,0:T(8,128)(2,1)}, bf16[1,4,16,256]{3,2,1,0:T(8,128)(2,1)}, bf16[1,4,16...) while((s32[]{:T(128)}, bf16[16,2048]{1,0:T(8,128)(2,1)S(1)}, ...), condition=%wide.wide.region_14.15_spmd, body=%wide.wide.region_1.14_spmd.sunk | while | flops 1262831360 | bytes 25890184 | solution.py:209
  67.1 1.3 select_dynamic-update-slice_fusion.4
  70.9 2.1 fusion.157
  74.3 1.7 fusion.162
  78.7 18.7 %all_to_all.49 = bf16[8,16,2048]{2,1,0:T(8,128)(2,1)S(1)} all-to-all(bf16[8,16,2048]{2,1,0:T(8,128)(2,1)S(1)} %fusion.165), channel_id=1, replica_groups=mesh['section'=4,'expert'=8] {'expert'}, dimensions={0} | all-to-all | bytes 1048576 | tf_op jit(solution)/shard_map/while/body/eval_jaxpr/all_to_all | solution.py:135
  99.5 5.2 %fusion.167 = bf16[128,2048]{1,0:T(8,128)(2,1)} fusion(bf16[1,1,768,2048]{3,2,1,0:T(8,128)(2,1)} %get-tuple-element.921, bf16[128,2048]{1,0:T(8,128)(2,1)} %bitcast.161, bf16[1,1,2048,768]{3,2,1,0:T(8,128)(2,1)} %get-tuple-element.920, f32[128,768]{1,0:T(8,128)} %fusion.166), kind=kOutput, calls=%fused_computation.8.clone.clone.1 | convolution fusion | flops 806158336 | bytes 7733248 | tf_op jit(solution)/shard_map/while/body/eval_jaxpr/dot_general | solution.py:28
  104.7 4.3 all-to-all-start.1
  109.3 13.4 %all-to-all-done.1 = bf16[8,16,2048]{2,1,0:T(8,128)(2,1)} async-done(((bf16[8,16,2048]{2,1,0:T(8,128)(2,1)}), bf16[8,16,2048]{2,1,0:T(8,128)(2,1)}, u32[]{:S(2)}, u32[]{:S(2)}) %all-to-all-start.1) | async-done | bytes 524320 | tf_op jit(solution)/shard_map/while/body/eval_jaxpr/all_to_all | solution.py:142
  122.6 1.4 convolution_bitcast_fusion.3
  124.5 1.6 fusion.169
  133.5 2.1 fusion.157
  136.8 1.7 fusion.162
  141.3 18.6 %all_to_all.49 = bf16[8,16,2048]{2,1,0:T(8,128)(2,1)S(1)} all-to-all(bf16[8,16,2048]{2,1,0:T(8,128)(2,1)S(1)} %fusion.165), channel_id=1, replica_groups=mesh['section'=4,'expert'=8] {'expert'}, dimensions={0} | all-to-all | bytes 1048576 | tf_op jit(solution)/shard_map/while/body/eval_jaxpr/all_to_all | solution.py:135
  162.0 5.2 %fusion.167 = bf16[128,2048]{1,0:T(8,128)(2,1)} fusion(bf16[1,1,768,2048]{3,2,1,0:T(8,128)(2,1)} %get-tuple-element.921, bf16[128,2048]{1,0:T(8,128)(2,1)} %bitcast.161, bf16[1,1,2048,768]{3,2,1,0:T(8,128)(2,1)} %get-tuple-element.920, f32[128,768]{1,0:T(8,128)} %fusion.166), kind=kOutput, calls=%fused_computation.8.clone.clone.1 | convolution fusion | flops 806158336 | bytes 7733248 | tf_op jit(solution)/shard_map/while/body/eval_jaxpr/dot_general | solution.py:28
  167.2 4.4 all-to-all-start.1
  171.9 15.1 %all-to-all-done.1 = bf16[8,16,2048]{2,1,0:T(8,128)(2,1)} async-done(((bf16[8,16,2048]{2,1,0:T(8,128)(2,1)}), bf16[8,16,2048]{2,1,0:T(8,128)(2,1)}, u32[]{:S(2)}, u32[]{:S(2)}) %all-to-all-start.1) | async-done | bytes 524320 | tf_op jit(solution)/shard_map/while/body/eval_jaxpr/all_to_all | solution.py:142
  187.0 1.4 convolution_bitcast_fusion.3
  188.8 1.6 fusion.169
  190.4 1.4 collective-permute-start
  197.9 2.1 fusion.157
  201.3 1.7 fusion.162
  205.7 19.1 %all_to_all.49 = bf16[8,16,2048]{2,1,0:T(8,128)(2,1)S(1)} all-to-all(bf16[8,16,2048]{2,1,0:T(8,128)(2,1)S(1)} %fusion.165), channel_id=1, replica_groups=mesh['section'=4,'expert'=8] {'expert'}, dimensions={0} | all-to-all | bytes 1048576 | tf_op jit(solution)/shard_map/while/body/eval_jaxpr/all_to_all | solution.py:135
  226.9 5.2 %fusion.167 = bf16[128,2048]{1,0:T(8,128)(2,1)} fusion(bf16[1,1,768,2048]{3,2,1,0:T(8,128)(2,1)} %get-tuple-element.921, bf16[128,2048]{1,0:T(8,128)(2,1)} %bitcast.161, bf16[1,1,2048,768]{3,2,1,0:T(8,128)(2,1)} %get-tuple-element.920, f32[128,768]{1,0:T(8,128)} %fusion.166), kind=kOutput, calls=%fused_computation.8.clone.clone.1 | convolution fusion | flops 806158336 | bytes 7733248 | tf_op jit(solution)/shard_map/while/body/eval_jaxpr/dot_general | solution.py:28
  232.1 4.3 all-to-all-start.1
  236.7 14.0 %all-to-all-done.1 = bf16[8,16,2048]{2,1,0:T(8,128)(2,1)} async-done(((bf16[8,16,2048]{2,1,0:T(8,128)(2,1)}), bf16[8,16,2048]{2,1,0:T(8,128)(2,1)}, u32[]{:S(2)}, u32[]{:S(2)}) %all-to-all-start.1) | async-done | bytes 524320 | tf_op jit(solution)/shard_map/while/body/eval_jaxpr/all_to_all | solution.py:142
  250.7 1.4 convolution_bitcast_fusion.3
  252.5 1.6 fusion.169
  261.5 2.1 fusion.157
  264.9 1.7 fusion.162
  269.3 19.0 %all_to_all.49 = bf16[8,16,2048]{2,1,0:T(8,128)(2,1)S(1)} all-to-all(bf16[8,16,2048]{2,1,0:T(8,128)(2,1)S(1)} %fusion.165), channel_id=1, replica_groups=mesh['section'=4,'expert'=8] {'expert'}, dimensions={0} | all-to-all | bytes 1048576 | tf_op jit(solution)/shard_map/while/body/eval_jaxpr/all_to_all | solution.py:135
  290.5 5.2 %fusion.167 = bf16[128,2048]{1,0:T(8,128)(2,1)} fusion(bf16[1,1,768,2048]{3,2,1,0:T(8,128)(2,1)} %get-tuple-element.921, bf16[128,2048]{1,0:T(8,128)(2,1)} %bitcast.161, bf16[1,1,2048,768]{3,2,1,0:T(8,128)(2,1)} %get-tuple-element.920, f32[128,768]{1,0:T(8,128)} %fusion.166), kind=kOutput, calls=%fused_computation.8.clone.clone.1 | convolution fusion | flops 806158336 | bytes 7733248 | tf_op jit(solution)/shard_map/while/body/eval_jaxpr/dot_general | solution.py:28
  295.7 4.3 all-to-all-start.1
  300.2 14.0 %all-to-all-done.1 = bf16[8,16,2048]{2,1,0:T(8,128)(2,1)} async-done(((bf16[8,16,2048]{2,1,0:T(8,128)(2,1)}), bf16[8,16,2048]{2,1,0:T(8,128)(2,1)}, u32[]{:S(2)}, u32[]{:S(2)}) %all-to-all-start.1) | async-done | bytes 524320 | tf_op jit(solution)/shard_map/while/body/eval_jaxpr/all_to_all | solution.py:142
  314.2 1.4 convolution_bitcast_fusion.3
  316.1 1.6 fusion.169
  325.1 2.1 fusion.157
  328.4 1.7 fusion.162
  332.9 19.0 %all_to_all.49 = bf16[8,16,2048]{2,1,0:T(8,128)(2,1)S(1)} all-to-all(bf16[8,16,2048]{2,1,0:T(8,128)(2,1)S(1)} %fusion.165), channel_id=1, replica_groups=mesh['section'=4,'expert'=8] {'expert'}, dimensions={0} | all-to-all | bytes 1048576 | tf_op jit(solution)/shard_map/while/body/eval_jaxpr/all_to_all | solution.py:135
  354.0 5.2 %fusion.167 = bf16[128,2048]{1,0:T(8,128)(2,1)} fusion(bf16[1,1,768,2048]{3,2,1,0:T(8,128)(2,1)} %get-tuple-element.921, bf16[128,2048]{1,0:T(8,128)(2,1)} %bitcast.161, bf16[1,1,2048,768]{3,2,1,0:T(8,128)(2,1)} %get-tuple-element.920, f32[128,768]{1,0:T(8,128)} %fusion.166), kind=kOutput, calls=%fused_computation.8.clone.clone.1 | convolution fusion | flops 806158336 | bytes 7733248 | tf_op jit(solution)/shard_map/while/body/eval_jaxpr/dot_general | solution.py:28
  359.2 4.3 all-to-all-start.1
  363.7 14.0 %all-to-all-done.1 = bf16[8,16,2048]{2,1,0:T(8,128)(2,1)} async-done(((bf16[8,16,2048]{2,1,0:T(8,128)(2,1)}), bf16[8,16,2048]{2,1,0:T(8,128)(2,1)}, u32[]{:S(2)}, u32[]{:S(2)}) %all-to-all-start.1) | async-done | bytes 524320 | tf_op jit(solution)/shard_map/while/body/eval_jaxpr/all_to_all | solution.py:142
  377.7 1.4 convolution_bitcast_fusion.3
  379.6 1.6 fusion.169
  388.6 2.1 fusion.157
  391.9 1.7 fusion.162
  396.4 19.0 %all_to_all.49 = bf16[8,16,2048]{2,1,0:T(8,128)(2,1)S(1)} all-to-all(bf16[8,16,2048]{2,1,0:T(8,128)(2,1)S(1)} %fusion.165), channel_id=1, replica_groups=mesh['section'=4,'expert'=8] {'expert'}, dimensions={0} | all-to-all | bytes 1048576 | tf_op jit(solution)/shard_map/while/body/eval_jaxpr/all_to_all | solution.py:135
  417.5 5.2 %fusion.167 = bf16[128,2048]{1,0:T(8,128)(2,1)} fusion(bf16[1,1,768,2048]{3,2,1,0:T(8,128)(2,1)} %get-tuple-element.921, bf16[128,2048]{1,0:T(8,128)(2,1)} %bitcast.161, bf16[1,1,2048,768]{3,2,1,0:T(8,128)(2,1)} %get-tuple-element.920, f32[128,768]{1,0:T(8,128)} %fusion.166), kind=kOutput, calls=%fused_computation.8.clone.clone.1 | convolution fusion | flops 806158336 | bytes 7733248 | tf_op jit(solution)/shard_map/while/body/eval_jaxpr/dot_general | solution.py:28
  422.7 4.3 all-to-all-start.1
  427.3 14.0 %all-to-all-done.1 = bf16[8,16,2048]{2,1,0:T(8,128)(2,1)} async-done(((bf16[8,16,2048]{2,1,0:T(8,128)(2,1)}), bf16[8,16,2048]{2,1,0:T(8,128)(2,1)}, u32[]{:S(2)}, u32[]{:S(2)}) %all-to-all-start.1) | async-done | bytes 524320 | tf_op jit(solution)/shard_map/while/body/eval_jaxpr/all_to_all | solution.py:142
  441.3 1.4 convolution_bitcast_fusion.3
  443.1 1.6 fusion.169
  452.1 2.1 fusion.157
  455.5 1.7 fusion.162
  459.9 19.0 %all_to_all.49 = bf16[8,16,2048]{2,1,0:T(8,128)(2,1)S(1)} all-to-all(bf16[8,16,2048]{2,1,0:T(8,128)(2,1)S(1)} %fusion.165), channel_id=1, replica_groups=mesh['section'=4,'expert'=8] {'expert'}, dimensions={0} | all-to-all | bytes 1048576 | tf_op jit(solution)/shard_map/while/body/eval_jaxpr/all_to_all | solution.py:135
  481.0 5.2 %fusion.167 = bf16[128,2048]{1,0:T(8,128)(2,1)} fusion(bf16[1,1,768,2048]{3,2,1,0:T(8,128)(2,1)} %get-tuple-element.921, bf16[128,2048]{1,0:T(8,128)(2,1)} %bitcast.161, bf16[1,1,2048,768]{3,2,1,0:T(8,128)(2,1)} %get-tuple-element.920, f32[128,768]{1,0:T(8,128)} %fusion.166), kind=kOutput, calls=%fused_computation.8.clone.clone.1 | convolution fusion | flops 806158336 | bytes 7733248 | tf_op jit(solution)/shard_map/while/body/eval_jaxpr/dot_general | solution.py:28
  486.2 4.3 all-to-all-start.1
  490.8 14.0 %all-to-all-done.1 = bf16[8,16,2048]{2,1,0:T(8,128)(2,1)} async-done(((bf16[8,16,2048]{2,1,0:T(8,128)(2,1)}), bf16[8,16,2048]{2,1,0:T(8,128)(2,1)}, u32[]{:S(2)}, u32[]{:S(2)}) %all-to-all-start.1) | async-done | bytes 524320 | tf_op jit(solution)/shard_map/while/body/eval_jaxpr/all_to_all | solution.py:142
  504.8 1.4 convolution_bitcast_fusion.3
  506.6 1.6 fusion.169
  (424 shorter events, 101.1 us)
Async XLA Ops:
  6.5 57.1 %all-reduce.2.cloned.1.call-start = ((), (), s32[]{:S(2)}) async-start(), calls=%async_computation.3 | async-start | bytes 524288 | tf_op jit(solution)/shard_map/psum | solution.py:107
  15.2 50.4 %copy-start = (bf16[1,1,2048,768]{3,2,1,0:T(8,128)(2,1)S(1)}, bf16[1,1,2048,768]{3,2,1,0:T(8,128)(2,1)}, u32[]{:S(2)}) copy-start(bf16[1,1,2048,768]{3,2,1,0:T(8,128)(2,1)} %param.27) | copy-start | bytes 9437188
  15.3 50.4 %copy-start.6 = (f32[1,2048]{1,0:T(1,128)S(1)}, f32[1,2048]{1,0:T(1,128)}, u32[]{:S(2)}) copy-start(f32[1,2048]{1,0:T(1,128)} %param.18) | copy-start | bytes 24580
  15.3 50.4 %copy-start.9 = (f32[1,2,128]{2,1,0:T(2,128)S(1)}, f32[1,2,128]{2,1,0:T(2,128)}, u32[]{:S(2)}) copy-start(f32[1,2,128]{2,1,0:T(2,128)} %param.21) | copy-start | bytes 3076
  66.9 6.2 %copy-start.11 = (pred[4]{0:T(512)(128)(4,1)}, pred[4]{0:T(512)(128)(4,1)S(1)}, u32[]{:S(2)}) copy-start(pred[4]{0:T(512)(128)(4,1)S(1)} %iota_compare_fusion.9) | copy-start | bytes 16 | tf_op jit(solution)/shard_map/while
  67.0 3.8 copy-start.2
  74.3 4.0 copy-start.5
  99.5 9.5 %copy-start.8 = (f32[1,4,128,4]{2,3,1,0:T(4,128)S(1)}, f32[1,4,128,4]{2,3,1,0:T(4,128)}, u32[]{:S(2)}) copy-start(f32[1,4,128,4]{2,3,1,0:T(4,128)} %get-tuple-element.917) | copy-start | bytes 24580 | tf_op jit(solution)/shard_map/while
  104.7 23.5 %copy-start.7 = (f32[1,2048]{1,0:T(1,128)S(1)}, f32[1,2048]{1,0:T(1,128)}, u32[]{:S(2)}) copy-start(f32[1,2048]{1,0:T(1,128)} %get-tuple-element.964) | copy-start | bytes 24580 | tf_op jit(solution)/shard_map/while
  104.7 23.5 %copy-start.10 = (f32[1,2,128]{2,1,0:T(2,128)S(1)}, f32[1,2,128]{2,1,0:T(2,128)}, u32[]{:S(2)}) copy-start(f32[1,2,128]{2,1,0:T(2,128)} %get-tuple-element.993) | copy-start | bytes 3076 | tf_op jit(solution)/shard_map/while
  104.7 17.9 %all-to-all-start.1 = ((bf16[8,16,2048]{2,1,0:T(8,128)(2,1)}), bf16[8,16,2048]{2,1,0:T(8,128)(2,1)}, u32[]{:S(2)}, u32[]{:S(2)}) async-start(bf16[8,16,2048]{2,1,0:T(8,128)(2,1)} %bitcast.167), calls=%async_computation.1 | async-start | bytes 1048576 | tf_op jit(solution)/shard_map/while/body/eval_jaxpr/all_to_all | solution.py:142
  126.0 2.2 collective-permute-start
  129.5 6.2 %copy-start.11 = (pred[4]{0:T(512)(128)(4,1)}, pred[4]{0:T(512)(128)(4,1)S(1)}, u32[]{:S(2)}) copy-start(pred[4]{0:T(512)(128)(4,1)S(1)} %iota_compare_fusion.9) | copy-start | bytes 16 | tf_op jit(solution)/shard_map/while
  129.6 3.8 copy-start.2
  132.5 3.5 copy-start.4
  136.8 4.0 copy-start.5
  162.0 9.6 %copy-start.8 = (f32[1,4,128,4]{2,3,1,0:T(4,128)S(1)}, f32[1,4,128,4]{2,3,1,0:T(4,128)}, u32[]{:S(2)}) copy-start(f32[1,4,128,4]{2,3,1,0:T(4,128)} %get-tuple-element.917) | copy-start | bytes 24580 | tf_op jit(solution)/shard_map/while
  167.2 25.5 %copy-start.7 = (f32[1,2048]{1,0:T(1,128)S(1)}, f32[1,2048]{1,0:T(1,128)}, u32[]{:S(2)}) copy-start(f32[1,2048]{1,0:T(1,128)} %get-tuple-element.964) | copy-start | bytes 24580 | tf_op jit(solution)/shard_map/while
  167.2 25.5 %copy-start.10 = (f32[1,2,128]{2,1,0:T(2,128)S(1)}, f32[1,2,128]{2,1,0:T(2,128)}, u32[]{:S(2)}) copy-start(f32[1,2,128]{2,1,0:T(2,128)} %get-tuple-element.993) | copy-start | bytes 3076 | tf_op jit(solution)/shard_map/while
  167.2 19.8 %all-to-all-start.1 = ((bf16[8,16,2048]{2,1,0:T(8,128)(2,1)}), bf16[8,16,2048]{2,1,0:T(8,128)(2,1)}, u32[]{:S(2)}, u32[]{:S(2)}) async-start(bf16[8,16,2048]{2,1,0:T(8,128)(2,1)} %bitcast.167), calls=%async_computation.1 | async-start | bytes 1048576 | tf_op jit(solution)/shard_map/while/body/eval_jaxpr/all_to_all | solution.py:142
  190.4 2.3 collective-permute-start
  193.9 6.2 %copy-start.11 = (pred[4]{0:T(512)(128)(4,1)}, pred[4]{0:T(512)(128)(4,1)S(1)}, u32[]{:S(2)}) copy-start(pred[4]{0:T(512)(128)(4,1)S(1)} %iota_compare_fusion.9) | copy-start | bytes 16 | tf_op jit(solution)/shard_map/while
  194.0 3.8 copy-start.2
  196.9 3.5 copy-start.4
  201.3 4.0 copy-start.5
  226.9 9.5 %copy-start.8 = (f32[1,4,128,4]{2,3,1,0:T(4,128)S(1)}, f32[1,4,128,4]{2,3,1,0:T(4,128)}, u32[]{:S(2)}) copy-start(f32[1,4,128,4]{2,3,1,0:T(4,128)} %get-tuple-element.917) | copy-start | bytes 24580 | tf_op jit(solution)/shard_map/while
  232.1 24.2 %copy-start.7 = (f32[1,2048]{1,0:T(1,128)S(1)}, f32[1,2048]{1,0:T(1,128)}, u32[]{:S(2)}) copy-start(f32[1,2048]{1,0:T(1,128)} %get-tuple-element.964) | copy-start | bytes 24580 | tf_op jit(solution)/shard_map/while
  232.1 24.2 %copy-start.10 = (f32[1,2,128]{2,1,0:T(2,128)S(1)}, f32[1,2,128]{2,1,0:T(2,128)}, u32[]{:S(2)}) copy-start(f32[1,2,128]{2,1,0:T(2,128)} %get-tuple-element.993) | copy-start | bytes 3076 | tf_op jit(solution)/shard_map/while
  232.1 18.6 %all-to-all-start.1 = ((bf16[8,16,2048]{2,1,0:T(8,128)(2,1)}), bf16[8,16,2048]{2,1,0:T(8,128)(2,1)}, u32[]{:S(2)}, u32[]{:S(2)}) async-start(bf16[8,16,2048]{2,1,0:T(8,128)(2,1)} %bitcast.167), calls=%async_computation.1 | async-start | bytes 1048576 | tf_op jit(solution)/shard_map/while/body/eval_jaxpr/all_to_all | solution.py:142
  254.1 2.2 collective-permute-start
  257.5 6.2 %copy-start.11 = (pred[4]{0:T(512)(128)(4,1)}, pred[4]{0:T(512)(128)(4,1)S(1)}, u32[]{:S(2)}) copy-start(pred[4]{0:T(512)(128)(4,1)S(1)} %iota_compare_fusion.9) | copy-start | bytes 16 | tf_op jit(solution)/shard_map/while
  257.7 3.8 copy-start.2
  260.6 3.5 copy-start.4
  264.9 4.0 copy-start.5
  290.5 9.5 %copy-start.8 = (f32[1,4,128,4]{2,3,1,0:T(4,128)S(1)}, f32[1,4,128,4]{2,3,1,0:T(4,128)}, u32[]{:S(2)}) copy-start(f32[1,4,128,4]{2,3,1,0:T(4,128)} %get-tuple-element.917) | copy-start | bytes 24580 | tf_op jit(solution)/shard_map/while
  295.7 24.2 %copy-start.7 = (f32[1,2048]{1,0:T(1,128)S(1)}, f32[1,2048]{1,0:T(1,128)}, u32[]{:S(2)}) copy-start(f32[1,2048]{1,0:T(1,128)} %get-tuple-element.964) | copy-start | bytes 24580 | tf_op jit(solution)/shard_map/while
  295.7 24.2 %copy-start.10 = (f32[1,2,128]{2,1,0:T(2,128)S(1)}, f32[1,2,128]{2,1,0:T(2,128)}, u32[]{:S(2)}) copy-start(f32[1,2,128]{2,1,0:T(2,128)} %get-tuple-element.993) | copy-start | bytes 3076 | tf_op jit(solution)/shard_map/while
  295.7 18.6 %all-to-all-start.1 = ((bf16[8,16,2048]{2,1,0:T(8,128)(2,1)}), bf16[8,16,2048]{2,1,0:T(8,128)(2,1)}, u32[]{:S(2)}, u32[]{:S(2)}) async-start(bf16[8,16,2048]{2,1,0:T(8,128)(2,1)} %bitcast.167), calls=%async_computation.1 | async-start | bytes 1048576 | tf_op jit(solution)/shard_map/while/body/eval_jaxpr/all_to_all | solution.py:142
  317.6 2.2 collective-permute-start
  321.1 6.2 %copy-start.11 = (pred[4]{0:T(512)(128)(4,1)}, pred[4]{0:T(512)(128)(4,1)S(1)}, u32[]{:S(2)}) copy-start(pred[4]{0:T(512)(128)(4,1)S(1)} %iota_compare_fusion.9) | copy-start | bytes 16 | tf_op jit(solution)/shard_map/while
  321.2 3.8 copy-start.2
  328.4 4.0 copy-start.5
  354.0 9.5 %copy-start.8 = (f32[1,4,128,4]{2,3,1,0:T(4,128)S(1)}, f32[1,4,128,4]{2,3,1,0:T(4,128)}, u32[]{:S(2)}) copy-start(f32[1,4,128,4]{2,3,1,0:T(4,128)} %get-tuple-element.917) | copy-start | bytes 24580 | tf_op jit(solution)/shard_map/while
  359.2 24.2 %copy-start.7 = (f32[1,2048]{1,0:T(1,128)S(1)}, f32[1,2048]{1,0:T(1,128)}, u32[]{:S(2)}) copy-start(f32[1,2048]{1,0:T(1,128)} %get-tuple-element.964) | copy-start | bytes 24580 | tf_op jit(solution)/shard_map/while
  359.2 24.2 %copy-start.10 = (f32[1,2,128]{2,1,0:T(2,128)S(1)}, f32[1,2,128]{2,1,0:T(2,128)}, u32[]{:S(2)}) copy-start(f32[1,2,128]{2,1,0:T(2,128)} %get-tuple-element.993) | copy-start | bytes 3076 | tf_op jit(solution)/shard_map/while
  359.2 18.6 %all-to-all-start.1 = ((bf16[8,16,2048]{2,1,0:T(8,128)(2,1)}), bf16[8,16,2048]{2,1,0:T(8,128)(2,1)}, u32[]{:S(2)}, u32[]{:S(2)}) async-start(bf16[8,16,2048]{2,1,0:T(8,128)(2,1)} %bitcast.167), calls=%async_computation.1 | async-start | bytes 1048576 | tf_op jit(solution)/shard_map/while/body/eval_jaxpr/all_to_all | solution.py:142
  381.2 2.2 collective-permute-start
  384.6 6.2 %copy-start.11 = (pred[4]{0:T(512)(128)(4,1)}, pred[4]{0:T(512)(128)(4,1)S(1)}, u32[]{:S(2)}) copy-start(pred[4]{0:T(512)(128)(4,1)S(1)} %iota_compare_fusion.9) | copy-start | bytes 16 | tf_op jit(solution)/shard_map/while
  384.7 3.8 copy-start.2
  387.6 3.5 copy-start.4
  391.9 4.0 copy-start.5
  417.5 9.5 %copy-start.8 = (f32[1,4,128,4]{2,3,1,0:T(4,128)S(1)}, f32[1,4,128,4]{2,3,1,0:T(4,128)}, u32[]{:S(2)}) copy-start(f32[1,4,128,4]{2,3,1,0:T(4,128)} %get-tuple-element.917) | copy-start | bytes 24580 | tf_op jit(solution)/shard_map/while
  422.7 24.2 %copy-start.7 = (f32[1,2048]{1,0:T(1,128)S(1)}, f32[1,2048]{1,0:T(1,128)}, u32[]{:S(2)}) copy-start(f32[1,2048]{1,0:T(1,128)} %get-tuple-element.964) | copy-start | bytes 24580 | tf_op jit(solution)/shard_map/while
  422.7 24.2 %copy-start.10 = (f32[1,2,128]{2,1,0:T(2,128)S(1)}, f32[1,2,128]{2,1,0:T(2,128)}, u32[]{:S(2)}) copy-start(f32[1,2,128]{2,1,0:T(2,128)} %get-tuple-element.993) | copy-start | bytes 3076 | tf_op jit(solution)/shard_map/while
  422.7 18.6 %all-to-all-start.1 = ((bf16[8,16,2048]{2,1,0:T(8,128)(2,1)}), bf16[8,16,2048]{2,1,0:T(8,128)(2,1)}, u32[]{:S(2)}, u32[]{:S(2)}) async-start(bf16[8,16,2048]{2,1,0:T(8,128)(2,1)} %bitcast.167), calls=%async_computation.1 | async-start | bytes 1048576 | tf_op jit(solution)/shard_map/while/body/eval_jaxpr/all_to_all | solution.py:142
  444.7 2.2 collective-permute-start
  448.1 6.2 %copy-start.11 = (pred[4]{0:T(512)(128)(4,1)}, pred[4]{0:T(512)(128)(4,1)S(1)}, u32[]{:S(2)}) copy-start(pred[4]{0:T(512)(128)(4,1)S(1)} %iota_compare_fusion.9) | copy-start | bytes 16 | tf_op jit(solution)/shard_map/while
  448.2 3.8 copy-start.2
  455.5 4.0 copy-start.5
  481.0 9.5 %copy-start.8 = (f32[1,4,128,4]{2,3,1,0:T(4,128)S(1)}, f32[1,4,128,4]{2,3,1,0:T(4,128)}, u32[]{:S(2)}) copy-start(f32[1,4,128,4]{2,3,1,0:T(4,128)} %get-tuple-element.917) | copy-start | bytes 24580 | tf_op jit(solution)/shard_map/while
  486.2 24.2 %copy-start.7 = (f32[1,2048]{1,0:T(1,128)S(1)}, f32[1,2048]{1,0:T(1,128)}, u32[]{:S(2)}) copy-start(f32[1,2048]{1,0:T(1,128)} %get-tuple-element.964) | copy-start | bytes 24580 | tf_op jit(solution)/shard_map/while
  486.2 24.2 %copy-start.10 = (f32[1,2,128]{2,1,0:T(2,128)S(1)}, f32[1,2,128]{2,1,0:T(2,128)}, u32[]{:S(2)}) copy-start(f32[1,2,128]{2,1,0:T(2,128)} %get-tuple-element.993) | copy-start | bytes 3076 | tf_op jit(solution)/shard_map/while
  486.2 18.6 %all-to-all-start.1 = ((bf16[8,16,2048]{2,1,0:T(8,128)(2,1)}), bf16[8,16,2048]{2,1,0:T(8,128)(2,1)}, u32[]{:S(2)}, u32[]{:S(2)}) async-start(bf16[8,16,2048]{2,1,0:T(8,128)(2,1)} %bitcast.167), calls=%async_computation.1 | async-start | bytes 1048576 | tf_op jit(solution)/shard_map/while/body/eval_jaxpr/all_to_all | solution.py:142
  508.2 2.2 collective-permute-start
  (17 other events, 32.0 us)
Sparse Core Ops, SparseCore 0:
  32.6 30.9 all-reduce.1
where the time goes:
time: 522 us; the launch traced here: 517 us
  blocking collectives  149 us (29%)
  waiting for transfers between devices  131 us (25%)
  matrix products  102 us (20%)
  other arithmetic  42.2 us (8%)
  starting transfers between devices  39.1 us (7%)
  local copies, waits for them, and re-layouts  38.3 us (7%)
  between operations  13.5 us (3%)
    all_to_all x7, blocking collectives, expert_mix(): lax.all_to_all(outgoing, 'expert', split_axis=0, concat_axis=0, tiled=True)  132 us
    all_to_all x7, waiting for transfers between devices, expert_mix(): lax.all_to_all(served, 'expert', split_axis=0, concat_axis=0, tiled=True)  98.5 us
    dot_general x7, matrix products, expert_block(): jnp.dot(activated, down_matrix, preferred_element_type=jnp.float32)  36.4 us
    all_to_all x7, starting transfers between devices, expert_mix(): lax.all_to_all(served, 'expert', split_axis=0, concat_axis=0, tiled=True)  30 us
    psum x1, waiting for transfers between devices, on_device(): lax.psum(owned_rows.astype(jnp.float32).astype(jnp.bfloat16), 'section')  26.8 us
    all_to_all x1, blocking collectives, on_device(): lax.all_to_all(looked, 'expert', split_axis=1, concat_axis=2, tiled=True)  16.2 us
    dot_general x7, matrix products, attend(): jnp.einsum('rgjd,rcgd->rgjc', queries, key_grid, preferred_element_type=j...  14.6 us
    dot_general x7, matrix products, attend(): jnp.einsum('rgjc,rcgd->rgjd', far_probs, value_grid, preferred_element_ty...  11.7 us
  transfers between devices with their start and end apart: 15, of which 15 were waited for; matrix products, arithmetic and copies ran while one was open for 1% of the time, Pallas kernels for 0%

commit v1 on v0

v1 whole, which is shorter than its diff:
```python
import functools
import math

import jax
import jax.numpy as jnp
from jax import lax
from jax.experimental import pallas as pl
from jax.experimental.pallas import tpu as pltpu
from jax.sharding import PartitionSpec as P

GROUPS = 1
EPS = 1e-06
NEG = -1e30
MESH = pl.DeviceIdType.MESH
F32 = jnp.float32
BF16 = jnp.bfloat16


def layers_kernel(
    n_sec, n_exp, n_groups, dims,
    looked, far_live, shares, attn_gain, moe_gain, query_gain, key_gain,
    keys_hbm, values_hbm, gate_hbm, up_hbm, down_hbm,
    out,
    keys, values, gate, up, down,
    emb_land, h_in, near_k, near_v, qn, att, mid,
    x_land, act, y, p_land, q_land,
    load_sem, emb_send, emb_recv, h_send, h_recv,
    ag_send, fwd_send, ag_recv, p_send, p_recv, q_send, q_recv,
):
    rows, steps, width, head, kv, blocks, ff = dims
    part = width // n_exp
    nz = n_exp // 2
    per = steps // n_groups
    count = per * rows
    total = 2 * nz * count
    sec = lax.axis_index("section")
    me = lax.axis_index("expert")
    z, x = me // 2, me % 2
    partner = z * 2 + (1 - x)
    last = n_sec - 1

    loads = [
        pltpu.make_async_copy(src, dst, load_sem.at[i])
        for i, (src, dst) in enumerate(
            [(keys_hbm, keys), (values_hbm, values), (gate_hbm, gate), (up_hbm, up), (down_hbm, down)]
        )
    ]
    for load in loads:
        load.start()

    def peer(k):
        return lax.rem(z + k, nz)

    barrier = pltpu.get_barrier_semaphore()

    def greet(section, expert):
        pl.semaphore_signal(
            barrier, inc=1, device_id={"section": section, "expert": expert}, device_id_type=MESH
        )

    for k in range(1, nz):
        greet(sec, peer(k) * 2 + x)
    greet(sec, partner)

    @pl.when(sec > 0)
    def _():
        greet(sec - 1, me)
        for k in range(n_exp):
            greet(0, k)

    @pl.when(sec < last)
    def _():
        greet(sec + 1, me)

    @pl.when(sec == 0)
    def _():
        for k in range(1, n_exp):
            greet(0, lax.rem(me + k, n_exp))
        for s in range(1, n_sec):
            for k in range(n_exp):
                greet(s, k)

    @pl.when(sec == 0)
    def _():
        pl.semaphore_wait(barrier, nz + n_exp * n_sec)

    @pl.when((sec > 0) & (sec < last))
    def _():
        pl.semaphore_wait(barrier, nz + n_exp + 2)

    @pl.when(sec == last)
    def _():
        pl.semaphore_wait(barrier, nz + n_exp + 1)

    def emb_copy(k):
        to = lax.rem(me + k, n_exp)
        return pltpu.make_async_remote_copy(
            src_ref=looked.at[to], dst_ref=emb_land.at[sec, me],
            send_sem=emb_send, recv_sem=emb_recv,
            device_id={"section": 0, "expert": to}, device_id_type=MESH,
        )

    for k in range(1, n_exp):
        emb_copy(k).start()

    @pl.when(sec > 0)
    def _():
        emb_copy(0).start()

    near_k[...] = jnp.zeros_like(near_k)
    near_v[...] = jnp.zeros_like(near_v)

    @pl.when(sec == 0)
    def _():
        own = pltpu.make_async_copy(looked.at[me], emb_land.at[0, me], emb_recv)
        own.start()
        pltpu.make_async_copy(emb_land, emb_land, emb_recv).wait()
        for g in range(n_groups):
            for e in range(n_exp):
                whole = emb_land[0, e, g * count:(g + 1) * count, :].astype(F32)
                for s in range(1, n_sec):
                    whole = whole + emb_land[s, e, g * count:(g + 1) * count, :].astype(F32)
                h_in[g, :, e * part:(e + 1) * part] = whole.astype(BF16)

    def h_copy(g):
        return pltpu.make_async_remote_copy(
            src_ref=out.at[g], dst_ref=h_in.at[g],
            send_sem=h_send.at[g], recv_sem=h_recv.at[g],
            device_id={"section": sec + 1, "expert": me}, device_id_type=MESH,
        )

    def ag_copy(g, k):
        return pltpu.make_async_remote_copy(
            src_ref=x_land.at[g, 0, z], dst_ref=x_land.at[g, 0, z],
            send_sem=ag_send.at[g, k], recv_sem=ag_recv.at[g, 0, z],
            device_id={"section": sec, "expert": peer(k) * 2 + x}, device_id_type=MESH,
        )

    def fwd_copy(g, k):
        at = peer(k)
        return pltpu.make_async_remote_copy(
            src_ref=x_land.at[g, 0, at], dst_ref=x_land.at[g, 1, at],
            send_sem=fwd_send.at[g, k], recv_sem=ag_recv.at[g, 1, at],
            device_id={"section": sec, "expert": partner}, device_id_type=MESH,
        )

    def p_copy(g, k):
        at = peer(k)
        return pltpu.make_async_remote_copy(
            src_ref=y.at[g, 1, at], dst_ref=p_land.at[g, at],
            send_sem=p_send.at[g, k], recv_sem=p_recv.at[g, at],
            device_id={"section": sec, "expert": partner}, device_id_type=MESH,
        )

    def q_copy(g, k):
        at = peer(k)
        return pltpu.make_async_remote_copy(
            src_ref=y.at[g, 0, at], dst_ref=q_land.at[g, z],
            send_sem=q_send.at[g, k], recv_sem=q_recv.at[g, z],
            device_id={"section": sec, "expert": at * 2 + x}, device_id_type=MESH,
        )

    def landed(ref, sem):
        pltpu.make_async_copy(ref, ref, sem).wait()

    def cut(j, size=head):
        return slice(j * size, (j + 1) * size)

    scale = 1.0 / math.sqrt(head)
    contract = (((1,), (1,)), ((), ()))
    q_rows = per * blocks

    for g in range(n_groups):
        @pl.when(sec > 0)
        def _():
            landed(h_in.at[g], h_recv.at[g])

        square = jnp.zeros((count, head), F32)
        for j in range(blocks):
            piece = h_in[g, :, cut(j)].astype(F32)
            square = square + piece * piece
        factor = lax.rsqrt(jnp.sum(square, axis=-1, keepdims=True) / width + EPS)
        for j in range(blocks):
            piece = h_in[g, :, cut(j)].astype(F32) * factor * attn_gain[:, cut(j)]
            normed = piece * lax.rsqrt(jnp.mean(piece * piece, axis=-1, keepdims=True) + EPS)
            qn[pl.ds(j, count, stride=blocks), :] = normed
            here = slice(g * count, (g + 1) * count)
            if j < kv:
                near_k[here, cut(j)] = (normed * key_gain[j:j + 1, :]).astype(BF16)
            elif j < 2 * kv:
                near_v[here, cut(j - kv)] = piece.astype(BF16)

        if g == 0:
            loads[0].wait()
            loads[1].wait()

        spot = lax.broadcasted_iota(jnp.int32, (q_rows, steps * rows), 1)
        step_of = lax.broadcasted_iota(jnp.int32, (q_rows, steps * rows), 0) // blocks + g * per
        causal = spot // rows <= step_of
        spot_row = spot % rows

        def one_row(r):
            starts = [pl.multiple_of((t * rows + r) * blocks, blocks) for t in range(per)]
            base = jnp.concatenate([qn[pl.ds(at, blocks), :] for at in starts], axis=0)
            live = far_live[pl.ds(r, 1), :] > 0.5
            near_live = causal & (spot_row == r)
            mixed = None
            for h in range(kv):
                gain = query_gain[h * blocks:(h + 1) * blocks, :]
                query = (base * jnp.concatenate([gain] * per, axis=0)).astype(BF16)
                far = lax.dot_general(
                    query, keys[r, :, cut(h)], contract, preferred_element_type=F32) * scale
                near = lax.dot_general(
                    query, near_k[:, cut(h)], contract, preferred_element_type=F32) * scale
                far = jnp.where(live, far, NEG)
                near = jnp.where(near_live, near, NEG)
                top = jnp.maximum(
                    jnp.max(far, axis=-1, keepdims=True), jnp.max(near, axis=-1, keepdims=True))
                far = jnp.exp(far - top)
                near = jnp.exp(near - top)
                inverse = 1.0 / (
                    jnp.sum(far, axis=-1, keepdims=True) + jnp.sum(near, axis=-1, keepdims=True))
                part_out = jnp.dot(
                    (far * inverse).astype(BF16), values[r, :, cut(h)], preferred_element_type=F32)
                part_out += jnp.dot(
                    (near * inverse).astype(BF16), near_v[:, cut(h)], preferred_element_type=F32)
                mixed = part_out if mixed is None else mixed + part_out
            for t in range(per):
                att[pl.ds(starts[t], blocks), :] = mixed[t * blocks:(t + 1) * blocks, :]

        @pl.loop(0, rows // 4)
        def _(quad):
            for i in range(4):
                one_row(quad * 4 + i)

        square = jnp.zeros((count, head), F32)
        for j in range(blocks):
            piece = h_in[g, :, cut(j)].astype(F32) + att[pl.ds(j, count, stride=blocks), :]
            mid[:, cut(j)] = piece
            square = square + piece * piece
        factor = lax.rsqrt(jnp.sum(square, axis=-1, keepdims=True) / width + EPS)
        for j in range(blocks):
            x_land[g, 0, z, :, cut(j)] = (mid[:, cut(j)] * factor * moe_gain[:, cut(j)]).astype(BF16)

        for k in range(1, nz):
            ag_copy(g, k).start()
        fwd_copy(g, 0).start()
        for k in range(1, nz):
            landed(x_land.at[g, 0, peer(k)], ag_recv.at[g, 0, peer(k)])
            fwd_copy(g, k).start()
        for k in range(nz):
            landed(x_land.at[g, 1, peer(k)], ag_recv.at[g, 1, peer(k)])

        if g == 0:
            for load in loads[2:]:
                load.wait()

        chunk = min(total, 512)
        per_chunk = chunk // count

        for c in range(total // chunk):
            line, first = c * per_chunk // nz, c * per_chunk % nz
            if per_chunk <= nz:
                rows_in = x_land[g, line, first:first + per_chunk].reshape(chunk, width)
            else:
                rows_in = x_land[g].reshape(chunk, width)
            share = shares[g, c * chunk:(c + 1) * chunk, :]

            @pl.loop(0, ff // 256)
            def _(i):
                at = pl.ds(pl.multiple_of(i * 256, 256), 256)
                gate_part = jnp.dot(rows_in, gate[:, at], preferred_element_type=F32)
                lifted = jnp.dot(rows_in, up[:, at], preferred_element_type=F32)
                act[:, at] = (gate_part / (1.0 + jnp.exp(-gate_part)) * lifted).astype(BF16)

            @pl.loop(0, width // 256)
            def _(i):
                at = pl.ds(pl.multiple_of(i * 256, 256), 256)
                served = jnp.dot(act[...], down[:, at], preferred_element_type=F32).astype(BF16)
                term = (served.astype(F32) * share).astype(BF16)
                if per_chunk <= nz:
                    y[g, line, first:first + per_chunk, :, at] = term.reshape(per_chunk, count, 256)
                else:
                    y[g, :, :, :, at] = term.reshape(2, nz, count, 256)

        for k in list(range(1, nz)) + [0]:
            p_copy(g, k).start()
        for k in range(1, nz):
            at = peer(k)
            landed(p_land.at[g, at], p_recv.at[g, at])
            y[g, 0, at] = (y[g, 0, at].astype(F32) + p_land[g, at].astype(F32)).astype(BF16)
            q_copy(g, k).start()
        landed(p_land.at[g, z], p_recv.at[g, z])
        for j in range(blocks):
            piece = y[g, 0, z, :, cut(j)].astype(F32) + p_land[g, z, :, cut(j)].astype(F32)
            mid[:, cut(j)] = mid[:, cut(j)] + piece
        for k in range(1, nz):
            landed(q_land.at[g, peer(k)], q_recv.at[g, peer(k)])
        for j in range(blocks):
            piece = mid[:, cut(j)]
            for k in range(1, nz):
                piece = piece + q_land[g, peer(k), :, cut(j)].astype(F32)
            out[g, :, cut(j)] = piece.astype(BF16)

        @pl.when(sec < last)
        def _():
            h_copy(g).start()

    @pl.when(sec == 0)
    def _():
        landed(emb_land.at[0, pl.ds(0, n_exp - 1)], emb_send)

    @pl.when(sec > 0)
    def _():
        landed(emb_land.at[0], emb_send)

    for g in range(n_groups):
        for k in range(1, nz):
            ag_copy(g, k).wait_send()
            q_copy(g, k).wait_send()
        for k in range(nz):
            fwd_copy(g, k).wait_send()
            p_copy(g, k).wait_send()

        @pl.when(sec < last)
        def _():
            h_copy(g).wait_send()


def on_device(
    token_ids, embed_table, attn_gain, moe_gain, query_gain, key_gain, key_cache, value_cache,
    cache_len, expert_ids, route_raw, gate_weights, up_weights, down_weights,
):
    n_sec = lax.axis_size("section")
    n_exp = lax.axis_size("expert")
    sec = lax.axis_index("section")
    me = lax.axis_index("expert")
    steps, all_rows = token_ids.shape
    vocab_part, part = embed_table.shape
    rows = all_rows // n_exp
    width = attn_gain.shape[1]
    head = query_gain.shape[2]
    kv = key_gain.shape[1]
    blocks = width // head
    cache = key_cache.shape[2]
    ff = gate_weights.shape[3]
    nz = n_exp // 2
    groups = GROUPS
    per = steps // groups
    count = per * rows

    ordered = token_ids.reshape(steps, n_exp, rows).transpose(1, 0, 2).reshape(n_exp, steps * rows)
    shifted = ordered - sec * vocab_part
    inside = (shifted >= 0) & (shifted < vocab_part)
    looked = jnp.take(embed_table, jnp.clip(shifted, 0, vocab_part - 1), axis=0)
    looked = jnp.where(inside[:, :, None], looked, jnp.zeros_like(looked))

    far_live = (jnp.arange(cache)[None, :] < cache_len[:, None]).astype(F32)
    weights = route_raw[0] / jnp.sum(route_raw[0], axis=-1, keepdims=True)
    share = jnp.sum(jnp.where(expert_ids[0] == me, weights, 0.0), axis=-1)
    share = share.reshape(groups, per, nz, 2, rows).transpose(0, 3, 2, 1, 4)
    share = jnp.where(me % 2 == 0, share, share[:, ::-1])
    share = share.reshape(groups, 2 * nz * count, 1)

    dims = (rows, steps, width, head, kv, blocks, ff)
    vmem = pl.BlockSpec(memory_space=pltpu.VMEM)
    hbm = pl.BlockSpec(memory_space=pl.ANY)
    dma = pltpu.SemaphoreType.DMA
    out = pl.pallas_call(
        functools.partial(layers_kernel, n_sec, n_exp, groups, dims),
        out_shape=jax.ShapeDtypeStruct((groups, count, width), BF16),
        in_specs=[vmem] * 7 + [hbm] * 5,
        out_specs=vmem,
        scratch_shapes=[
            pltpu.VMEM(key_cache.shape[1:], BF16),
            pltpu.VMEM(key_cache.shape[1:], BF16),
            pltpu.VMEM((width, ff), BF16),
            pltpu.VMEM((width, ff), BF16),
            pltpu.VMEM((ff, width), BF16),
            pltpu.VMEM((n_sec, n_exp, steps * rows, part), BF16),
            pltpu.VMEM((groups, count, width), BF16),
            pltpu.VMEM((steps * rows, kv * head), BF16),
            pltpu.VMEM((steps * rows, kv * head), BF16),
            pltpu.VMEM((count * blocks, head), F32),
            pltpu.VMEM((count * blocks, head), F32),
            pltpu.VMEM((count, width), F32),
            pltpu.VMEM((groups, 2, nz, count, width), BF16),
            pltpu.VMEM((min(2 * nz * count, 512), ff), BF16),
            pltpu.VMEM((groups, 2, nz, count, width), BF16),
            pltpu.VMEM((groups, nz, count, width), BF16),
            pltpu.VMEM((groups, nz, count, width), BF16),
            dma((5,)), dma, dma, dma((groups,)), dma((groups,)),
            dma((groups, nz)), dma((groups, nz)), dma((groups, 2, nz)),
            dma((groups, nz)), dma((groups, nz)), dma((groups, nz)), dma((groups, nz)),
        ],
        compiler_params=pltpu.CompilerParams(
            collective_id=0, has_side_effects=True, vmem_limit_bytes=60 * 2**20
        ),
    )(
        looked, far_live, share, attn_gain, moe_gain, query_gain[0], key_gain[0],
        key_cache[0], value_cache[0], gate_weights[0, 0], up_weights[0, 0], down_weights[0, 0],
    )
    return out.reshape(1, steps, rows, width)


def solution(mesh):
    in_specs = (
        P(),
        P("section", "expert"),
        P("section", None),
        P("section", None),
        P("section", None, None),
        P("section", None, None),
        P("section", "expert", None, None),
        P("section", "expert", None, None),
        P("expert"),
        P("section", None, None, None),
        P("section", None, None, None),
        P("section", "expert", None, None),
        P("section", "expert", None, None),
        P("section", "expert", None, None),
    )
    out_specs = P("section", None, "expert", None)
    return jax.shard_map(
        on_device, mesh=mesh, in_specs=in_specs, out_specs=out_specs, check_vma=False
    )
```

time: 522 us -> 275 us (0.53)
  the two profiles are of different devices: /device:TPU:0 before, /device:TPU:5 now
where the time goes in v1:
time: 275 us; the launch traced here: 274 us
  Pallas kernels  260 us (95%)
  local copies, waits for them, and re-layouts  9.78 us (4%)
  other arithmetic  4.45 us (2%)
    pallas_call x1, Pallas kernels, on_device(): pl.pallas_call(functools.partial(layers_kernel, n_sec, n_exp, groups, dim...  260 us
    gather x1, local copies, waits for them, and re-layouts, on_device(): looked = jnp.take(embed_table, jnp.clip(shifted, 0, vocab_part - 1), axis=0)  6.6 us

profile of v1, /device:TPU:5, one launch (start us, length us, event | category | flops | bytes accessed | tf_op | source)
XLA Modules:
  0.0 273.9 jit_solution(2460017320129910826)
XLA Ops:
  0.0 0.0 copy-start
  0.0 0.7 reduce_sum.18
  0.7 0.7 fusion
  1.5 0.1 reshape.78
  1.6 0.9 reshape.91.shares
  2.5 0.7 subtract_clamp_fusion
  3.2 0.1 min.20
  3.3 0.1 min.24
  3.4 0.1 reshape.84
  3.5 6.6 %gather_fusion = bf16[512,256]{1,0:T(8,128)(2,1)S(1)} fusion(bf16[18992,256]{1,0:T(8,128)(2,1)} %param.15, s32[1024]{0:T(1024)S(1)} %pad_clamp_fusion), kind=kCustom, calls=%fused_computation | custom fusion | bytes 526336 | tf_op jit(solution)/shard_map/jit(_take)/gather | solution.py:355
  10.1 0.1 min.22
  10.2 0.7 compare_and_fusion.1
  10.8 0.1 reshape.81
  10.9 0.1 and.29
  11.0 0.9 select_select_fusion.looked
  11.9 0.0 copy-done
  12.0 0.7 fusion.1.far_live
  12.6 259.6 %shard_map.136 = bf16[1,64,2048]{2,1,0:T(8,128)(2,1)} custom-call(bf16[8,64,256]{2,1,0:T(8,128)(2,1)} %select_select_fusion.looked, f32[16,128]{1,0:T(8,128)} %fusion.1.far_live, f32[1,512,1]{2,1,0:T(8,128)} %reshape.91.shares, f32[1,2048]{1,0:T(1,128)} %attn_gain.1, f32[1,2048]{1,0:T(1,128)} %moe_gain.1, f32[32,128]{1,0:T(8,128)} %bitcast.33, ...), custom_call_target="tpu_custom_call" | custom-call | tf_op jit(solution)/shard_map/pallas_call | solution.py:369
  272.2 1.7 copy.24
  (8 shorter events, 0.1 us)
Async XLA Ops:
  0.0 12.0 %copy-start = (s32[16]{0:T(128)S(1)}, s32[16]{0:T(128)}, u32[]{:S(2)}) copy-start(s32[16]{0:T(128)} %param.22) | copy-start | bytes 196

commit v2 on v1

v2 whole, which is shorter than its diff:
```python
import functools
import math

import jax
import jax.numpy as jnp
from jax import lax
from jax.experimental import pallas as pl
from jax.experimental.pallas import tpu as pltpu
from jax.sharding import PartitionSpec as P

GROUPS = 4
EPS = 1e-06
NEG = -1e30
MESH = pl.DeviceIdType.MESH
F32 = jnp.float32
BF16 = jnp.bfloat16


def layers_kernel(
    n_sec, n_exp, n_groups, dims,
    looked, far_live, shares, attn_gain, moe_gain, query_gain, key_gain,
    keys_hbm, values_hbm, gate_hbm, up_hbm, down_hbm,
    out,
    keys, values, gate, up, down,
    emb_land, h_in, near_k, near_v, qn, att, mid,
    x_land, act, y, p_land, q_land,
    load_sem, emb_send, emb_recv, h_send, h_recv,
    ag_send, fwd_send, ag_recv, p_send, p_recv, q_send, q_recv,
):
    rows, steps, width, head, kv, blocks, ff, cache = dims
    part = width // n_exp
    nz = n_exp // 2
    per = steps // n_groups
    count = per * rows
    total = 2 * nz * count
    sec = lax.axis_index("section")
    me = lax.axis_index("expert")
    z, x = me // 2, me % 2
    partner = z * 2 + (1 - x)
    last = n_sec - 1

    loads = [
        pltpu.make_async_copy(src, dst, load_sem.at[i])
        for i, (src, dst) in enumerate(
            [(keys_hbm, keys.at[:, 0:cache]), (values_hbm, values.at[:, 0:cache]), (gate_hbm, gate), (up_hbm, up), (down_hbm, down)]
        )
    ]
    for load in loads:
        load.start()

    def peer(k):
        return lax.rem(z + k, nz)

    barrier = pltpu.get_barrier_semaphore()

    def greet(section, expert):
        pl.semaphore_signal(
            barrier, inc=1, device_id={"section": section, "expert": expert}, device_id_type=MESH
        )

    for k in range(1, nz):
        greet(sec, peer(k) * 2 + x)
    greet(sec, partner)

    @pl.when(sec > 0)
    def _():
        greet(sec - 1, me)
        for k in range(n_exp):
            greet(0, k)

    @pl.when(sec < last)
    def _():
        greet(sec + 1, me)

    @pl.when(sec == 0)
    def _():
        for k in range(1, n_exp):
            greet(0, lax.rem(me + k, n_exp))
        for s in range(1, n_sec):
            for k in range(n_exp):
                greet(s, k)

    @pl.when(sec == 0)
    def _():
        pl.semaphore_wait(barrier, nz + n_exp * n_sec)

    @pl.when((sec > 0) & (sec < last))
    def _():
        pl.semaphore_wait(barrier, nz + n_exp + 2)

    @pl.when(sec == last)
    def _():
        pl.semaphore_wait(barrier, nz + n_exp + 1)

    def emb_copy(g, k):
        to = lax.rem(me + k, n_exp)
        return pltpu.make_async_remote_copy(
            src_ref=looked.at[g, to], dst_ref=emb_land.at[g, sec, me],
            send_sem=emb_send.at[g], recv_sem=emb_recv.at[g],
            device_id={"section": 0, "expert": to}, device_id_type=MESH,
        )

    for g in range(n_groups):
        for k in range(1, n_exp):
            emb_copy(g, k).start()

        @pl.when(sec > 0)
        def _():
            emb_copy(g, 0).start()

        @pl.when(sec == 0)
        def _():
            pltpu.make_async_copy(looked.at[g, me], emb_land.at[g, 0, me], emb_recv.at[g]).start()

    near_k[...] = jnp.zeros_like(near_k)
    near_v[...] = jnp.zeros_like(near_v)

    def h_copy(g):
        return pltpu.make_async_remote_copy(
            src_ref=out.at[g], dst_ref=h_in.at[g],
            send_sem=h_send.at[g], recv_sem=h_recv.at[g],
            device_id={"section": sec + 1, "expert": me}, device_id_type=MESH,
        )

    def ag_copy(g, k):
        return pltpu.make_async_remote_copy(
            src_ref=x_land.at[g, 0, z], dst_ref=x_land.at[g, 0, z],
            send_sem=ag_send.at[g, k], recv_sem=ag_recv.at[g, 0, z],
            device_id={"section": sec, "expert": peer(k) * 2 + x}, device_id_type=MESH,
        )

    def fwd_copy(g, k):
        at = peer(k)
        return pltpu.make_async_remote_copy(
            src_ref=x_land.at[g, 0, at], dst_ref=x_land.at[g, 1, at],
            send_sem=fwd_send.at[g, k], recv_sem=ag_recv.at[g, 1, at],
            device_id={"section": sec, "expert": partner}, device_id_type=MESH,
        )

    def p_copy(g, k):
        at = peer(k)
        return pltpu.make_async_remote_copy(
            src_ref=y.at[g, 1, at], dst_ref=p_land.at[g, at],
            send_sem=p_send.at[g, k], recv_sem=p_recv.at[g, at],
            device_id={"section": sec, "expert": partner}, device_id_type=MESH,
        )

    def q_copy(g, k):
        at = peer(k)
        return pltpu.make_async_remote_copy(
            src_ref=y.at[g, 0, at], dst_ref=q_land.at[g, z],
            send_sem=q_send.at[g, k], recv_sem=q_recv.at[g, z],
            device_id={"section": sec, "expert": at * 2 + x}, device_id_type=MESH,
        )

    def landed(ref, sem):
        pltpu.make_async_copy(ref, ref, sem).wait()

    def cut(j, size=head):
        return slice(j * size, (j + 1) * size)

    scale = 1.0 / math.sqrt(head)
    contract = (((1,), (1,)), ((), ()))
    q_rows = per * blocks
    span = cache + 16

    def attention(g):
        @pl.when(sec == 0)
        def _():
            landed(emb_land.at[g], emb_recv.at[g])
            for e in range(n_exp):
                whole = emb_land[g, 0, e].astype(F32)
                for s in range(1, n_sec):
                    whole = whole + emb_land[g, s, e].astype(F32)
                h_in[g, :, e * part:(e + 1) * part] = whole.astype(BF16)

        @pl.when(sec > 0)
        def _():
            landed(h_in.at[g], h_recv.at[g])

        square = jnp.zeros((count, head), F32)
        for j in range(blocks):
            piece = h_in[g, :, cut(j)].astype(F32)
            square = square + piece * piece
        factor = lax.rsqrt(jnp.sum(square, axis=-1, keepdims=True) / width + EPS)
        for j in range(blocks):
            piece = h_in[g, :, cut(j)].astype(F32) * factor * attn_gain[:, cut(j)]
            normed = piece * lax.rsqrt(jnp.mean(piece * piece, axis=-1, keepdims=True) + EPS)
            qn[pl.ds(j, count, stride=blocks), :] = normed
            here = slice(g * count, (g + 1) * count)
            if j < kv:
                near_k[j, here, :] = normed * key_gain[j:j + 1, :]
            elif j < 2 * kv:
                near_v[j - kv, here, :] = piece

        if g == 0:
            loads[0].wait()
            loads[1].wait()

        spot = lax.broadcasted_iota(jnp.int32, (kv * q_rows, span), 1) - cache
        step_of = lax.broadcasted_iota(jnp.int32, (kv * q_rows, span), 0) % q_rows // blocks + g * per
        causal = (spot >= 0) & (spot <= step_of)
        gains = [
            jnp.concatenate([query_gain[h * blocks:(h + 1) * blocks, :]] * per, axis=0)
            for h in range(kv)
        ]
        blank = jnp.zeros((q_rows, head), BF16)
        fill = jnp.zeros((16 - steps, head), F32)

        def near_tile(ref, r):
            return jnp.concatenate(
                [
                    jnp.concatenate([ref[h, pl.ds(r, steps, stride=rows), :], fill], axis=0)
                    for h in range(kv)
                ],
                axis=1,
            ).astype(BF16)

        def one_row(r):
            starts = [pl.multiple_of((t * rows + r) * blocks, blocks) for t in range(per)]
            base = jnp.concatenate([qn[pl.ds(at, blocks), :] for at in starts], axis=0)
            keys[r, cache:span, :] = near_tile(near_k, r)
            values[r, cache:span, :] = near_tile(near_v, r)
            query = jnp.concatenate(
                [
                    jnp.concatenate(
                        [(base * gains[h]).astype(BF16) if i == h else blank for i in range(kv)],
                        axis=1,
                    )
                    for h in range(kv)
                ],
                axis=0,
            )
            live = (far_live[pl.ds(r, 1), :] > 0.5) | causal
            score = lax.dot_general(query, keys[r], contract, preferred_element_type=F32) * scale
            score = jnp.where(live, score, NEG)
            score = jnp.exp(score - jnp.max(score, axis=-1, keepdims=True))
            probs = (score * (1.0 / jnp.sum(score, axis=-1, keepdims=True))).astype(BF16)
            mixed = jnp.dot(probs, values[r], preferred_element_type=F32)
            both = mixed[:q_rows, :head]
            for h in range(1, kv):
                both = both + mixed[h * q_rows:(h + 1) * q_rows, h * head:(h + 1) * head]
            for t in range(per):
                att[pl.ds(starts[t], blocks), :] = both[t * blocks:(t + 1) * blocks, :]

        @pl.loop(0, rows // 8)
        def _(octet):
            for i in range(8):
                one_row(octet * 8 + i)

        square = jnp.zeros((count, head), F32)
        for j in range(blocks):
            piece = h_in[g, :, cut(j)].astype(F32) + att[pl.ds(j, count, stride=blocks), :]
            mid[g, :, cut(j)] = piece
            square = square + piece * piece
        factor = lax.rsqrt(jnp.sum(square, axis=-1, keepdims=True) / width + EPS)
        for j in range(blocks):
            x_land[g, 0, z, :, cut(j)] = (mid[g, :, cut(j)] * factor * moe_gain[:, cut(j)]).astype(BF16)

        for k in range(1, nz):
            ag_copy(g, k).start()
        fwd_copy(g, 0).start()

    def forward(g):
        for k in range(1, nz):
            landed(x_land.at[g, 0, peer(k)], ag_recv.at[g, 0, peer(k)])
            fwd_copy(g, k).start()

    def experts(g):
        for k in range(nz):
            landed(x_land.at[g, 1, peer(k)], ag_recv.at[g, 1, peer(k)])

        if g == 0:
            for load in loads[2:]:
                load.wait()

        rows_in = x_land[g].reshape(total, width)
        share = shares[g]

        @pl.loop(0, ff // 256)
        def _(i):
            at = pl.ds(pl.multiple_of(i * 256, 256), 256)
            gate_part = jnp.dot(rows_in, gate[:, at], preferred_element_type=F32)
            lifted = jnp.dot(rows_in, up[:, at], preferred_element_type=F32)
            act[:, at] = (gate_part / (1.0 + jnp.exp(-gate_part)) * lifted).astype(BF16)

        @pl.loop(0, width // 256)
        def _(i):
            at = pl.ds(pl.multiple_of(i * 256, 256), 256)
            served = jnp.dot(act[...], down[:, at], preferred_element_type=F32).astype(BF16)
            term = (served.astype(F32) * share).astype(BF16)
            y[g, :, :, :, at] = term.reshape(2, nz, count, 256)

        for k in list(range(1, nz)) + [0]:
            p_copy(g, k).start()

    def pair_up(g):
        for k in range(1, nz):
            at = peer(k)
            landed(p_land.at[g, at], p_recv.at[g, at])
            y[g, 0, at] = (y[g, 0, at].astype(F32) + p_land[g, at].astype(F32)).astype(BF16)
            q_copy(g, k).start()

    def finish(g):
        landed(p_land.at[g, z], p_recv.at[g, z])
        for k in range(1, nz):
            landed(q_land.at[g, peer(k)], q_recv.at[g, peer(k)])
        for j in range(blocks):
            piece = y[g, 0, z, :, cut(j)].astype(F32) + p_land[g, z, :, cut(j)].astype(F32)
            for k in range(1, nz):
                piece = piece + q_land[g, peer(k), :, cut(j)].astype(F32)
            out[g, :, cut(j)] = (mid[g, :, cut(j)] + piece).astype(BF16)

        @pl.when(sec < last)
        def _():
            h_copy(g).start()

    attention(0)
    for g in range(n_groups):
        forward(g)
        if g > 0:
            finish(g - 1)
        experts(g)
        if g + 1 < n_groups:
            attention(g + 1)
        pair_up(g)
    finish(n_groups - 1)

    @pl.when(sec == 0)
    def _():
        for g in range(n_groups):
            landed(emb_land.at[g, 0, pl.ds(0, n_exp - 1)], emb_send.at[g])

    @pl.when(sec > 0)
    def _():
        for g in range(n_groups):
            landed(emb_land.at[g, 0], emb_send.at[g])

    for g in range(n_groups):
        for k in range(1, nz):
            ag_copy(g, k).wait_send()
            q_copy(g, k).wait_send()
        for k in range(nz):
            fwd_copy(g, k).wait_send()
            p_copy(g, k).wait_send()

        @pl.when(sec < last)
        def _():
            h_copy(g).wait_send()


def on_device(
    token_ids, embed_table, attn_gain, moe_gain, query_gain, key_gain, key_cache, value_cache,
    cache_len, expert_ids, route_raw, gate_weights, up_weights, down_weights,
):
    n_sec = lax.axis_size("section")
    n_exp = lax.axis_size("expert")
    sec = lax.axis_index("section")
    me = lax.axis_index("expert")
    steps, all_rows = token_ids.shape
    vocab_part, part = embed_table.shape
    rows = all_rows // n_exp
    width = attn_gain.shape[1]
    head = query_gain.shape[2]
    kv = key_gain.shape[1]
    blocks = width // head
    cache = key_cache.shape[2]
    ff = gate_weights.shape[3]
    nz = n_exp // 2
    groups = GROUPS
    per = steps // groups
    count = per * rows

    ordered = token_ids.reshape(groups, per, n_exp, rows).transpose(0, 2, 1, 3)
    ordered = ordered.reshape(groups, n_exp, count)
    shifted = ordered - sec * vocab_part
    inside = (shifted >= 0) & (shifted < vocab_part)
    looked = jnp.take(embed_table, jnp.clip(shifted, 0, vocab_part - 1), axis=0)
    looked = jnp.where(inside[..., None], looked, jnp.zeros_like(looked))

    spots = jnp.arange(cache + 16)[None, :]
    far_live = ((spots < cache) & (spots < cache_len[:, None])).astype(F32)
    weights = route_raw[0] / jnp.sum(route_raw[0], axis=-1, keepdims=True)
    share = jnp.sum(jnp.where(expert_ids[0] == me, weights, 0.0), axis=-1)
    share = share.reshape(groups, per, nz, 2, rows).transpose(0, 3, 2, 1, 4)
    share = jnp.where(me % 2 == 0, share, share[:, ::-1])
    share = share.reshape(groups, 2 * nz * count, 1)

    dims = (rows, steps, width, head, kv, blocks, ff, cache)
    vmem = pl.BlockSpec(memory_space=pltpu.VMEM)
    hbm = pl.BlockSpec(memory_space=pl.ANY)
    dma = pltpu.SemaphoreType.DMA
    out = pl.pallas_call(
        functools.partial(layers_kernel, n_sec, n_exp, groups, dims),
        out_shape=jax.ShapeDtypeStruct((groups, count, width), BF16),
        in_specs=[vmem] * 7 + [hbm] * 5,
        out_specs=vmem,
        scratch_shapes=[
            pltpu.VMEM((rows, cache + 16, kv * head), BF16),
            pltpu.VMEM((rows, cache + 16, kv * head), BF16),
            pltpu.VMEM((width, ff), BF16),
            pltpu.VMEM((width, ff), BF16),
            pltpu.VMEM((ff, width), BF16),
            pltpu.VMEM((groups, n_sec, n_exp, count, part), BF16),
            pltpu.VMEM((groups, count, width), BF16),
            pltpu.VMEM((kv, steps * rows, head), F32),
            pltpu.VMEM((kv, steps * rows, head), F32),
            pltpu.VMEM((count * blocks, head), F32),
            pltpu.VMEM((count * blocks, head), F32),
            pltpu.VMEM((groups, count, width), F32),
            pltpu.VMEM((groups, 2, nz, count, width), BF16),
            pltpu.VMEM((2 * nz * count, ff), BF16),
            pltpu.VMEM((groups, 2, nz, count, width), BF16),
            pltpu.VMEM((groups, nz, count, width), BF16),
            pltpu.VMEM((groups, nz, count, width), BF16),
            dma((5,)), dma((groups,)), dma((groups,)), dma((groups,)), dma((groups,)),
            dma((groups, nz)), dma((groups, nz)), dma((groups, 2, nz)),
            dma((groups, nz)), dma((groups, nz)), dma((groups, nz)), dma((groups, nz)),
        ],
        compiler_params=pltpu.CompilerParams(
            collective_id=0, has_side_effects=True, vmem_limit_bytes=60 * 2**20
        ),
    )(
        looked, far_live, share, attn_gain, moe_gain, query_gain[0], key_gain[0],
        key_cache[0], value_cache[0], gate_weights[0, 0], up_weights[0, 0], down_weights[0, 0],
    )
    return out.reshape(1, steps, rows, width)


def solution(mesh):
    in_specs = (
        P(),
        P("section", "expert"),
        P("section", None),
        P("section", None),
        P("section", None, None),
        P("section", None, None),
        P("section", "expert", None, None),
        P("section", "expert", None, None),
        P("expert"),
        P("section", None, None, None),
        P("section", None, None, None),
        P("section", "expert", None, None),
        P("section", "expert", None, None),
        P("section", "expert", None, None),
    )
    out_specs = P("section", None, "expert", None)
    return jax.shard_map(
        on_device, mesh=mesh, in_specs=in_specs, out_specs=out_specs, check_vma=False
    )
```

time: 275 us -> 217 us (0.79)
  Pallas kernels: 260 us -> 203 us
    pallas_call x1, Pallas kernels: 260 us -> 203 us  [on_device(): pl.pallas_call(functools.partial(layers_kernel, n_sec, n_exp, groups, dim...]
where the time goes in v2:
time: 217 us
  Pallas kernels  203 us (94%)
  local copies, waits for them, and re-layouts  9.6 us (4%)
  other arithmetic  4.47 us (2%)
    pallas_call x1, Pallas kernels, on_device(): pl.pallas_call(functools.partial(layers_kernel, n_sec, n_exp, groups, dim...  203 us
    gather x1, local copies, waits for them, and re-layouts, on_device(): looked = jnp.take(embed_table, jnp.clip(shifted, 0, vocab_part - 1), axis=0)  6.6 us

profile of v2, /device:TPU:5, one launch (start us, length us, event | category | flops | bytes accessed | tf_op | source)
XLA Modules:
  0.0 216.9 jit_solution(3417602550829482013)
XLA Ops:
  0.0 0.0 copy-start
  0.0 0.7 reduce_sum.18
  0.7 0.7 fusion.2
  1.5 0.1 reshape.67
  1.6 0.9 reshape.79.shares
  2.5 0.7 subtract_clamp_fusion
  3.2 0.1 min.18
  3.3 0.1 reshape.72
  3.4 6.6 %gather_fusion = bf16[512,256]{1,0:T(8,128)(2,1)S(1)} fusion(bf16[18992,256]{1,0:T(8,128)(2,1)} %param.15, s32[1024]{0:T(1024)S(1)} %pad_clamp_fusion), kind=kCustom, calls=%fused_computation | custom fusion | bytes 526336 | tf_op jit(solution)/shard_map/jit(_take)/gather | solution.py:378
  10.0 0.1 min.16
  10.1 0.7 compare_and_fusion.1
  10.8 0.1 and.33
  10.9 0.9 select_select_fusion.looked
  11.8 0.0 copy-done
  11.8 0.7 fusion.1.far_live
  12.4 202.7 %shard_map.136 = bf16[4,16,2048]{2,1,0:T(8,128)(2,1)} custom-call(bf16[4,8,16,256]{3,2,1,0:T(8,128)(2,1)} %select_select_fusion.looked, f32[16,144]{1,0:T(8,128)} %fusion.1.far_live, f32[4,128,1]{2,1,0:T(8,128)} %reshape.79.shares, f32[1,2048]{1,0:T(1,128)} %attn_gain.1, f32[1,2048]{1,0:T(1,128)} %moe_gain.1, f32[32,128]{1,0:T(8,128)} %bitcast.31, ...), custom_call_target="tpu_custom_call" | custom-call | tf_op jit(solution)/shard_map/pallas_call | solution.py:393
  215.2 1.7 copy.18
  (7 shorter events, 0.1 us)
Async XLA Ops:
  0.0 11.8 %copy-start = (s32[16]{0:T(128)S(1)}, s32[16]{0:T(128)}, u32[]{:S(2)}) copy-start(s32[16]{0:T(128)} %param.22) | copy-start | bytes 196

commit v3 on v2

--- a/solution.py
+++ b/solution.py
@@ -257,14 +257,15 @@
         for j in range(blocks):
             x_land[g, 0, z, :, cut(j)] = (mid[g, :, cut(j)] * factor * moe_gain[:, cut(j)]).astype(BF16)
 
+        fwd_copy(g, 0).start()
         for k in range(1, nz):
             ag_copy(g, k).start()
-        fwd_copy(g, 0).start()
 
     def forward(g):
         for k in range(1, nz):
-            landed(x_land.at[g, 0, peer(k)], ag_recv.at[g, 0, peer(k)])
-            fwd_copy(g, k).start()
+            at = nz - k
+            landed(x_land.at[g, 0, peer(at)], ag_recv.at[g, 0, peer(at)])
+            fwd_copy(g, at).start()
 
     def experts(g):
         for k in range(nz):
@@ -277,19 +278,19 @@
         rows_in = x_land[g].reshape(total, width)
         share = shares[g]
 
-        @pl.loop(0, ff // 256)
+        @pl.loop(0, ff // 384)
         def _(i):
-            at = pl.ds(pl.multiple_of(i * 256, 256), 256)
+            at = pl.ds(pl.multiple_of(i * 384, 384), 384)
             gate_part = jnp.dot(rows_in, gate[:, at], preferred_element_type=F32)
             lifted = jnp.dot(rows_in, up[:, at], preferred_element_type=F32)
             act[:, at] = (gate_part / (1.0 + jnp.exp(-gate_part)) * lifted).astype(BF16)
 
-        @pl.loop(0, width // 256)
+        @pl.loop(0, width // 512)
         def _(i):
-            at = pl.ds(pl.multiple_of(i * 256, 256), 256)
+            at = pl.ds(pl.multiple_of(i * 512, 512), 512)
             served = jnp.dot(act[...], down[:, at], preferred_element_type=F32).astype(BF16)
             term = (served.astype(F32) * share).astype(BF16)
-            y[g, :, :, :, at] = term.reshape(2, nz, count, 256)
+            y[g, :, :, :, at] = term.reshape(2, nz, count, 512)
 
         for k in list(range(1, nz)) + [0]:
             p_copy(g, k).start()

time: 217 us -> 213 us (0.982)
  Pallas kernels: 203 us -> 198 us
    pallas_call x1, Pallas kernels: 203 us -> 198 us  [on_device(): pl.pallas_call(functools.partial(layers_kernel, n_sec, n_exp, groups, dim...]
where the time goes in v3:
time: 213 us
  Pallas kernels  198 us (93%)
  local copies, waits for them, and re-layouts  9.6 us (5%)
  other arithmetic  4.47 us (2%)
    pallas_call x1, Pallas kernels, on_device(): pl.pallas_call(functools.partial(layers_kernel, n_sec, n_exp, groups, dim...  198 us
    gather x1, local copies, waits for them, and re-layouts, on_device(): looked = jnp.take(embed_table, jnp.clip(shifted, 0, vocab_part - 1), axis=0)  6.6 us

profile of v3, /device:TPU:5, one launch (start us, length us, event | category | flops | bytes accessed | tf_op | source)
XLA Modules:
  0.0 212.6 jit_solution(17265931349420928936)
XLA Ops:
  0.0 0.0 copy-start
  0.0 0.7 reduce_sum.18
  0.7 0.7 fusion.2
  1.5 0.1 reshape.67
  1.6 0.9 reshape.79.shares
  2.5 0.7 subtract_clamp_fusion
  3.2 0.1 min.18
  3.3 0.1 reshape.72
  3.4 6.6 %gather_fusion = bf16[512,256]{1,0:T(8,128)(2,1)S(1)} fusion(bf16[18992,256]{1,0:T(8,128)(2,1)} %param.15, s32[1024]{0:T(1024)S(1)} %pad_clamp_fusion), kind=kCustom, calls=%fused_computation | custom fusion | bytes 526336 | tf_op jit(solution)/shard_map/jit(_take)/gather | solution.py:379
  10.0 0.1 min.16
  10.1 0.7 compare_and_fusion.1
  10.8 0.1 and.33
  10.9 0.9 select_select_fusion.looked
  11.8 0.0 copy-done
  11.8 0.7 fusion.1.far_live
  12.4 198.5 %shard_map.136 = bf16[4,16,2048]{2,1,0:T(8,128)(2,1)} custom-call(bf16[4,8,16,256]{3,2,1,0:T(8,128)(2,1)} %select_select_fusion.looked, f32[16,144]{1,0:T(8,128)} %fusion.1.far_live, f32[4,128,1]{2,1,0:T(8,128)} %reshape.79.shares, f32[1,2048]{1,0:T(1,128)} %attn_gain.1, f32[1,2048]{1,0:T(1,128)} %moe_gain.1, f32[32,128]{1,0:T(8,128)} %bitcast.31, ...), custom_call_target="tpu_custom_call" | custom-call | tf_op jit(solution)/shard_map/pallas_call | solution.py:394
  210.9 1.7 copy.18
  (7 shorter events, 0.1 us)
Async XLA Ops:
  0.0 11.8 %copy-start = (s32[16]{0:T(128)S(1)}, s32[16]{0:T(128)}, u32[]{:S(2)}) copy-start(s32[16]{0:T(128)} %param.22) | copy-start | bytes 196
